TPU v7x, 512 devices: a whole 4x4x16 slice. The times are simulated.
512 devices in a mesh: req: 64 (over y, z), head: 8 (over x, core).
Axes of the slice: x: 4, y: 4, z: 16, core: 2. Of those that a mesh axis runs over, the one named last changes fastest.
Arguments:
- tokens: bfloat16 [256, 2048], P('req'), may hold values from -1.1953125 to 1.1953125
- lengths: int32 [256], replicated, may hold values from 1 to 1021, as said below
- kv_cache: bfloat16 [1, 2, 65536, 8, 128], P(None, None, 'req', 'head'), may hold values from -24 to 24
- w_qkv: bfloat16 [1, 2048, 8, 512], P(None, 'req', 'head'), may hold values from -0.125 to 0.125
- w_headgate: bfloat16 [1, 2048, 16], P(None, None, 'head'), may hold values from -0.125 to 0.125
- w_out: bfloat16 [1, 2048, 2048], P(None, 'head', 'req'), may hold values from -0.5 to 0.5
- in_gain: float32 [1, 2048], replicated, may hold values from 0.5 to 1.5
- q_gain: float32 [1, 128], replicated, may hold values from 0.1 to 1.9
- k_gain: float32 [1, 128], replicated, may hold values from 0.1 to 1.9
- post_gain: float32 [1, 2048], replicated, may hold values from 0.5 to 1.5
- w_gate: bfloat16 [1, 2048, 6144], P(None, 'head', 'req'), may hold values from -0.125 to 0.125
- w_up: bfloat16 [1, 2048, 6144], P(None, 'head', 'req'), may hold values from -0.125 to 0.125
- w_down: bfloat16 [1, 6144, 2048], P(None, 'req', 'head'), may hold values from -0.078125 to 0.078125
- final_gain: float32 [2048], replicated, may hold values from 0.5 to 1.5
- w_vocab: bfloat16 [2048, 131072], P(None, ('req', 'head')), may hold values from -0.125 to 0.125
Outputs:
- logits: bfloat16 [256, 131072], P(None, ('req', 'head'))
Inputs may be any that keep to these rules, and one draw needn't show every extreme that they name: On every index of req the lengths of its 4 requests sum to at most 1024. On 8 indices, drawn anew, they sum to exactly 1024 and one request there is longer than 512; on one of these the other requests hold one token each. On every other index each length is at most 128 and one is exactly 128.
All inputs are finite; a program needn't handle non-finite values.
Results may differ from a plain program's by a relative error of at most 0.015.
Values may be sent and summed in bfloat16 or wider, within the bound.
No kernel may reach another device: no remote copies, remote signals or barrier semaphores. Data moves between devices by JAX's collectives and lax.ppermute only.
A program may use at most 64 MiB of HBM per device.

v0:
```python
import jax
import jax.numpy as jnp
from jax import lax
from jax.sharding import Mesh
from jax.sharding import PartitionSpec as P

EPSILON = 1e-06
ROPE_THETA = 1000000.0
Y, Z, X, C = (4, 16, 4, 2)
ZH, ZL = (4, 4)
DEPTH = ("zh", "zl")
F32, BF16 = (jnp.float32, jnp.bfloat16)


def rms_scale(values, gain):
    mean_square = jnp.mean(values * values, axis=-1, keepdims=True)
    return values * lax.rsqrt(mean_square + EPSILON) * gain


def rotate(values, cosine, sine):
    half = values.shape[-1] // 2
    a, b = (values[..., :half], values[..., half:])
    return jnp.concatenate([a * cosine - b * sine, b * cosine + a * sine], axis=-1)


def swap(values, axes):
    return lax.all_to_all(values, axes, split_axis=0, concat_axis=0, tiled=True)


def spread(values, axes, count):
    return swap(jnp.broadcast_to(values[None], (count,) + values.shape), axes)


def local(
    tokens,
    lengths,
    kv_cache,
    w_qkv,
    w_headgate,
    w_out,
    in_gain,
    q_gain,
    k_gain,
    post_gain,
    w_gate,
    w_up,
    w_down,
    final_gain,
    w_vocab,
):
    rows, width = tokens.shape
    head_dim = q_gain.shape[1]
    columns = w_qkv.shape[3]
    units = w_gate.shape[2]
    seg = width // (X * C)
    part_width = width // C
    req = lax.axis_index(("y",) + DEPTH)
    ix, ic = (lax.axis_index("x"), lax.axis_index("c"))
    ffn = jnp.concatenate([w_gate[0].T, w_up[0].T, w_down[0]], axis=0)
    ffn = lax.all_gather(ffn, ("y", "x"), axis=0).reshape(Y, X, -1, seg)
    qkv_block = lax.all_gather(w_qkv[0, :, 0], "y", axis=0, tiled=True)
    positions = lax.dynamic_slice_in_dim(lengths, req * rows, rows)
    starts = jnp.cumsum(positions) - positions
    limits = starts + positions
    token_wide = tokens.astype(F32)
    gained = (token_wide * in_gain[0]).astype(BF16)
    in_scale = lax.rsqrt(jnp.mean(token_wide * token_wide, axis=-1, keepdims=True) + EPSILON)
    normed = (token_wide * in_scale * in_gain[0]).astype(BF16)
    head_gate = jax.nn.sigmoid(jnp.dot(normed, w_headgate[0], preferred_element_type=F32))
    half = head_dim // 2
    frequency = ROPE_THETA ** (-2.0 * jnp.arange(half, dtype=F32) / head_dim)
    angles = positions.astype(F32)[:, None] * frequency[None, :]
    cosine, sine = (jnp.cos(angles), jnp.sin(angles))

    def own_row(array):
        return lax.dynamic_slice_in_dim(array, ix, 1, 0)

    def own_core(array, axis):
        return lax.dynamic_slice_in_dim(array, ic, 1, axis)

    residual = own_core(own_row(tokens).reshape(Y, C, seg), 1).reshape(8, head_dim)
    slot = jnp.arange(kv_cache.shape[2], dtype=jnp.int32)
    inside = (slot[None, :] >= starts[:, None]) & (slot[None, :] < limits[:, None])
    depth = width // (Y * Z)
    sent = gained.reshape(rows, Y, Z, depth).transpose(2, 0, 1, 3).reshape(Z, rows, Y * depth)
    block = w_out[0].T
    halves = [
        jnp.broadcast_to(
            block[None, :, q * head_dim : (q + 1) * head_dim], (Z, block.shape[0], head_dim)
        )
        for q in (0, 1)
    ]
    sent = jnp.concatenate([sent, jnp.zeros((Z, 8 - rows, head_dim), BF16)] + halves, axis=1)
    arrived = swap(sent, DEPTH)
    arrived, qkv_block, in_scale, head_gate, cosine, sine, residual, inside = (
        lax.optimization_barrier(
            (arrived, qkv_block, in_scale, head_gate, cosine, sine, residual, inside)
        )
    )
    batch = arrived[:, :rows].reshape(Z * rows, Y * depth)
    out_block = (
        arrived[:, 8:].reshape(Z, 2, -1, head_dim).transpose(1, 0, 2, 3).reshape(2, -1, head_dim)
    )
    part = jnp.dot(batch, qkv_block, preferred_element_type=F32).astype(BF16)
    part, out_block = lax.optimization_barrier((part.reshape(Z, rows, columns), out_block))
    part = swap(part, DEPTH)
    qkv = jnp.sum(part.astype(F32), axis=0) * in_scale
    query = qkv[:, : 2 * head_dim].reshape(rows, 2, head_dim)
    query = rotate(rms_scale(query, q_gain[0]), cosine[:, None], sine[:, None]).astype(BF16)
    key = qkv[:, 2 * head_dim : 3 * head_dim]
    key = rotate(rms_scale(key, k_gain[0]), cosine, sine).astype(BF16)
    value = qkv[:, 3 * head_dim :].astype(BF16)
    scale = head_dim ** (-0.5)
    keys, values = (kv_cache[0, 0, :, 0], kv_cache[0, 1, :, 0])
    score = jnp.einsum("rqd,sd->rqs", query, keys, preferred_element_type=F32) * scale
    weight = jnp.where(inside[:, None, :], jnp.exp(score), 0.0)
    own = jnp.exp(jnp.sum(query.astype(F32) * key.astype(F32)[:, None], axis=-1) * scale)
    total = jnp.sum(weight, axis=-1) + own
    summed = jnp.einsum("rqs,sd->rqd", weight.astype(BF16), values, preferred_element_type=F32)
    summed = summed + own.astype(BF16).astype(F32)[..., None] * value.astype(F32)[:, None]
    attended = summed / total[..., None]
    mixed = (attended * head_gate[..., None]).astype(BF16)
    everyone = spread(mixed.transpose(1, 0, 2).reshape(2 * rows, head_dim), "y", Y).reshape(
        Y, 2, rows, head_dim
    )
    part = jnp.einsum("yqrd,qnd->yrn", everyone, out_block, preferred_element_type=F32)
    part = swap(part.reshape(Y * rows * C, 2, head_dim), ("y", "x", "c"))
    projected = jnp.sum(part.reshape(Y, X * C, 2, head_dim), axis=1).reshape(8, head_dim)
    stream = (residual.astype(F32) + projected).astype(BF16)
    stream, post_gain = lax.optimization_barrier((stream, post_gain))
    post_half = own_core(post_gain.reshape(X, C, seg), 1).reshape(X, seg)
    gate_up = ffn[:, :, : 2 * units].transpose(1, 0, 2, 3)
    down = ffn[:, :, 2 * units :]
    batch, gate_up, down, post_half = lax.optimization_barrier(
        (spread(stream, DEPTH, Z), gate_up, down, post_half)
    )
    batch = batch.reshape(Z, X, seg)
    wide = batch.astype(F32)
    squares = jnp.sum(wide * wide, axis=(1, 2)).reshape(Z, 1)
    batch = (wide * post_half).astype(BF16)
    part = jnp.einsum("bxk,xyfk->byf", batch, gate_up, preferred_element_type=F32)
    part = jnp.concatenate([part.reshape(Z, -1), jnp.broadcast_to(squares, (Z, head_dim))], axis=1)
    both = jnp.sum(lax.all_gather(part, "c", axis=0), axis=0)
    scale = lax.rsqrt(both[:, -1:] / width + EPSILON)
    both = (both[:, :-head_dim] * scale).reshape(Z, Y, 2 * units)
    hidden = (jax.nn.silu(both[..., :units]) * both[..., units:]).astype(BF16)
    part = jnp.einsum("byf,yxfk->bxk", hidden, down, preferred_element_type=F32).astype(BF16)
    part = jnp.sum(spread(part.reshape(Z, 8, head_dim), "zl", ZL).astype(F32), axis=0).astype(BF16)
    lowered = jnp.sum(spread(part, "zh", ZH).astype(F32), axis=0)
    piece = (wide.reshape(Z, 8, head_dim) + lowered).astype(BF16).reshape(Z, part_width)
    near = spread(piece, ("y", "x"), Y * X).reshape(Y * X * Z, part_width)
    far = lax.ppermute(near, "c", [(0, 1), (1, 0)])
    near, far = (near.astype(F32), far.astype(F32))
    mean_square = (
        jnp.sum(near * near, axis=-1, keepdims=True) + jnp.sum(far * far, axis=-1, keepdims=True)
    ) / width
    scale = lax.rsqrt(mean_square + EPSILON)

    def scored(half, core):
        gain = lax.dynamic_slice_in_dim(final_gain.reshape(X, C, seg), core, 1, 1).reshape(
            1, part_width
        )
        vocab = lax.dynamic_slice_in_dim(w_vocab.reshape(X, C, seg, -1), core, 1, 1).reshape(
            part_width, -1
        )
        return jnp.dot((half * scale * gain).astype(BF16), vocab, preferred_element_type=F32)

    logits = (scored(near, ic) + scored(far, 1 - ic)).astype(BF16)
    logits = logits.reshape(Y, X, Z, w_vocab.shape[1]).transpose(0, 2, 1, 3)
    return logits.reshape(Y * X * Z, w_vocab.shape[1])


def solution(mesh):
    fine = Mesh(mesh.devices.reshape(Y, ZH, ZL, X, C), ("y", "zh", "zl", "x", "c"))
    req, head = (("y",) + DEPTH, ("x", "c"))
    in_specs = (
        P(req, None),
        P(),
        P(None, None, req, head, None),
        P(None, req, head, None),
        P(None, None, head),
        P(None, head, req),
        P(),
        P(),
        P(),
        P(),
        P(None, head, req),
        P(None, head, req),
        P(None, req, head),
        P(),
        P(None, req + head),
    )
    out_specs = P(None, req + head)
    return jax.shard_map(local, mesh=fine, in_specs=in_specs, out_specs=out_specs, check_vma=False)
```

profile of v0, /device:TPU:1, one launch (start us, length us, event | category | flops | bytes accessed | tf_op | source)
XLA Modules:
  0.0 161.6 jit_solution(16570574454729380939)
XLA Ops:
  6.6 0.8 fusion.47
  7.4 0.8 fusion.26
  8.2 0.1 reshape.221
  8.4 0.1 reshape.222
  8.5 0.1 pad.10.clone
  8.6 0.8 pad_maximum_fusion
  9.5 15.9 %all-to-all-start = ((bf16[16,72,128]{2,1,0:T(8,128)(2,1)}), bf16[16,72,128]{2,1,0:T(8,128)(2,1)S(1)}, u32[]{:S(2)}, u32[]{:S(2)}) async-start(bf16[16,72,128]{2,1,0:T(8,128)(2,1)} %pad_maximum_fusion), calls=%async_computation | async-start | bytes 589824 | tf_op jit(solution)/shard_map/all_to_all | solution.py:27
  25.4 0.7 pad_maximum_fusion.1
  26.2 0.1 dynamic-slice_bitcast_fusion
  26.2 0.2 reduce-window.8
  26.4 0.1 bitcast_subtract_fusion
  26.5 0.1 multiply_sine_fusion
  26.6 0.1 fusion.37
  26.8 10.4 %all-gather = bf16[1,128,1,512]{3,1,2,0:T(8,128)(2,1)S(1)} all-gather(bf16[1,32,1,512]{3,1,2,0:T(8,128)(2,1)S(1)} %copy-done.6), channel_id=2, replica_groups=mesh['y'=4,'zh'=4,'zl'=4,'x'=4,'c'=2] {'y'}, dimensions={1}, use_global_device_ids=true | all-gather | bytes 163840 | tf_op jit(solution)/shard_map/all_gather | solution.py:61
  37.2 0.2 fusion.10
  37.4 1.7 %all-to-all-done = bf16[16,72,128]{2,1,0:T(8,128)(2,1)S(1)} async-done(((bf16[16,72,128]{2,1,0:T(8,128)(2,1)}), bf16[16,72,128]{2,1,0:T(8,128)(2,1)S(1)}, u32[]{:S(2)}, u32[]{:S(2)}) %all-to-all-start) | async-done | bytes 294944 | tf_op jit(solution)/shard_map/all_to_all | solution.py:27
  39.2 0.1 convolution_convert_fusion
  39.4 23.1 %all_to_all.40 = bf16[16,4,512]{2,1,0:T(4,128)(2,1)S(1)} all-to-all(bf16[16,4,512]{2,1,0:T(4,128)(2,1)S(1)} %reshape.228), channel_id=1, replica_groups=mesh['y'=4,'zh'=4,'zl'=4,'x'=4,'c'=2] {'zh','zl'}, dimensions={0} | all-to-all | bytes 131072 | tf_op jit(solution)/shard_map/all_to_all | solution.py:27
  62.5 0.1 broadcast_multiply_fusion
  62.5 0.1 multiply_reduce_fusion.3
  62.7 0.1 multiply_multiply_fusion.1
  62.7 0.1 subtract_convert_fusion.1
  62.8 0.1 maximum_convert_fusion
  62.9 0.1 multiply_reduce_fusion.2
  63.0 0.1 multiply_multiply_fusion
  63.1 0.1 subtract_convert_fusion
  63.2 0.2 multiply_reduce_fusion.1
  63.3 0.3 fusion.48
  63.7 0.2 fusion.7
  63.8 8.2 %all_to_all.41 = bf16[4,8,128]{2,1,0:T(8,128)(2,1)S(1)} all-to-all(bf16[4,8,128]{2,1,0:T(8,128)(2,1)S(1)} %broadcast_in_dim.42), channel_id=1, replica_groups=mesh['y'=4,'zh'=4,'zl'=4,'x'=4,'c'=2] {'y'}, dimensions={0} | all-to-all | bytes 16384 | tf_op jit(solution)/shard_map/all_to_all | solution.py:27
  72.0 0.2 convolution_bitcast_fusion.2
  72.2 15.9 %all_to_all.42 = f32[32,2,128]{2,1,0:T(2,128)S(1)} all-to-all(f32[32,2,128]{2,1,0:T(2,128)S(1)} %reshape.233), channel_id=1, replica_groups=mesh['y'=4,'zh'=4,'zl'=4,'x'=4,'c'=2] {'y','x','c'}, dimensions={0} | all-to-all | bytes 65536 | tf_op jit(solution)/shard_map/all_to_all | solution.py:27
  88.2 0.6 broadcast_in_dim.43
  88.8 3.5 %all-to-all-start.4 = ((bf16[16,8,128]{2,1,0:T(8,128)(2,1)}), bf16[16,8,128]{2,1,0:T(8,128)(2,1)S(1)}, u32[]{:S(2)}, u32[]{:S(2)}) async-start(bf16[16,8,128]{2,1,0:T(8,128)(2,1)} %broadcast_in_dim.43), calls=%async_computation.4 | async-start | bytes 65536 | tf_op jit(solution)/shard_map/all_to_all | solution.py:27
  92.3 0.5 broadcast.164
  92.8 0.6 reduce.12
  93.5 1.5 slice_bitcast_fusion
  95.0 1.2 slice.85
  96.3 7.5 %all-to-all-done.4 = bf16[16,8,128]{2,1,0:T(8,128)(2,1)S(1)} async-done(((bf16[16,8,128]{2,1,0:T(8,128)(2,1)}), bf16[16,8,128]{2,1,0:T(8,128)(2,1)S(1)}, u32[]{:S(2)}, u32[]{:S(2)}) %all-to-all-start.4) | async-done | bytes 32800 | tf_op jit(solution)/shard_map/all_to_all | solution.py:27
  103.8 0.2 multiply_reduce_fusion
  104.0 0.1 copy.64
  104.2 0.5 convolution_bitcast_fusion.1
  104.7 0.1 broadcast_in_dim.44
  104.8 2.9 %all-gather.2 = f32[32,896]{1,0:T(8,128)S(1)} all-gather(f32[16,896]{1,0:T(8,128)S(1)} %pad_maximum_fusion.2), channel_id=4, replica_groups=mesh['y'=4,'zh'=4,'zl'=4,'x'=4,'c'=2] {'c'}, dimensions={0}, use_global_device_ids=true | all-gather | bytes 172032 | tf_op jit(solution)/shard_map/all_gather | solution.py:143
  107.7 0.2 fusion.40
  107.9 0.1 slice_multiply_fusion
  108.0 0.1 reshape.239
  108.1 0.1 fusion.46
  108.2 0.3 fusion.1
  108.5 7.4 %all_to_all.43 = bf16[4,16,8,128]{3,2,1,0:T(8,128)(2,1)S(1)} all-to-all(bf16[4,16,8,128]{3,2,1,0:T(8,128)(2,1)S(1)} %broadcast_in_dim.46), channel_id=1, replica_groups=mesh['y'=4,'zh'=4,'zl'=4,'x'=4,'c'=2] {'zl'}, dimensions={0} | all-to-all | bytes 262144 | tf_op jit(solution)/shard_map/all_to_all | solution.py:27
  116.0 15.6 %all_to_all.44 = bf16[4,16,8,128]{3,2,1,0:T(8,128)(2,1)S(1)} all-to-all(bf16[4,16,8,128]{3,2,1,0:T(8,128)(2,1)S(1)} %broadcast_in_dim.47), channel_id=1, replica_groups=mesh['y'=4,'zh'=4,'zl'=4,'x'=4,'c'=2] {'zh'}, dimensions={0} | all-to-all | bytes 262144 | tf_op jit(solution)/shard_map/all_to_all | solution.py:27
  131.7 11.8 %all_to_all.45 = bf16[16,16,1024]{2,1,0:T(8,128)(2,1)S(1)} all-to-all(bf16[16,16,1024]{2,1,0:T(8,128)(2,1)S(1)} %broadcast_in_dim.49), channel_id=1, replica_groups=mesh['y'=4,'zh'=4,'zl'=4,'x'=4,'c'=2] {'y','x'}, dimensions={0} | all-to-all | bytes 1048576 | tf_op jit(solution)/shard_map/all_to_all | solution.py:27
  143.5 7.9 %collective-permute-start = (bf16[256,1024]{1,0:T(8,128)(2,1)S(1)}, bf16[256,1024]{1,0:T(8,128)(2,1)S(1)}, u32[]{:S(2)}, u32[]{:S(2)}) collective-permute-start(bf16[256,1024]{1,0:T(8,128)(2,1)S(1)} %bitcast.122), channel_id=1, source_target_pairs={{0,1},{1,0},{2,3},{3,2},{4,5},{5,4},{6,7},{7,6},{8,9},{9,8},{10,11... | collective-permute-start | bytes 1572872 | tf_op jit(solution)/shard_map/ppermute | solution.py:152
  151.4 0.1 constant_dynamic-slice_fusion
  151.5 0.2 fusion.11
  151.7 0.1 reduce_sum.138
  151.7 1.1 collective-permute-done
  152.9 0.2 fusion.14
  153.0 0.1 reduce_sum.137
  153.1 0.2 fusion.13
  153.3 0.3 fusion.49
  153.7 0.4 fusion
  154.0 0.1 copy.69
  154.1 0.7 reshape.246
  (76 shorter events, 0.9 us)
Async XLA Ops:
  6.5 30.6 %copy-start = (bf16[1,2048,2]{1,2,0:T(2,128)(2,1)S(1)}, bf16[1,2048,2]{1,2,0:T(2,128)(2,1)}, u32[]{:S(2)}) copy-start(bf16[1,2048,2]{1,2,0:T(2,128)(2,1)} %param.19) | copy-start | bytes 24580
  6.5 20.2 %copy-start.5 = (bf16[4,2048]{1,0:T(4,128)(2,1)S(1)}, bf16[4,2048]{1,0:T(4,128)(2,1)}, u32[]{:S(2)}) copy-start(bf16[4,2048]{1,0:T(4,128)(2,1)} %param.15) | copy-start | bytes 49156
  6.5 30.6 %copy-start.9 = (f32[1,2048]{1,0:T(1,128)S(1)}, f32[1,2048]{1,0:T(1,128)}, u32[]{:S(2)}) copy-start(f32[1,2048]{1,0:T(1,128)} %param.21) | copy-start | bytes 24580
  6.5 18.9 %copy-start.2 = (bf16[1,96,256]{2,1,0:T(8,128)(2,1)S(1)}, bf16[1,96,256]{2,1,0:T(8,128)(2,1)}, u32[]{:S(2)}) copy-start(bf16[1,96,256]{2,1,0:T(8,128)(2,1)} %param.27) | copy-start | bytes 147460
  6.5 18.9 %copy-start.3 = (bf16[1,256,96]{1,2,0:T(8,128)(2,1)S(1)}, bf16[1,256,96]{1,2,0:T(8,128)(2,1)}, u32[]{:S(2)}) copy-start(bf16[1,256,96]{1,2,0:T(8,128)(2,1)} %param.26) | copy-start | bytes 147460
  6.5 18.9 %copy-start.4 = (bf16[1,256,96]{1,2,0:T(8,128)(2,1)S(1)}, bf16[1,256,96]{1,2,0:T(8,128)(2,1)}, u32[]{:S(2)}) copy-start(bf16[1,256,96]{1,2,0:T(8,128)(2,1)} %param.25) | copy-start | bytes 147460
  6.6 19.6 %copy-start.12 = (s32[256]{0:T(256)S(1)}, s32[256]{0:T(256)}, u32[]{:S(2)}) copy-start(s32[256]{0:T(256)} %param.16) | copy-start | bytes 3076
  6.6 20.3 %copy-start.6 = (bf16[1,32,1,512]{3,1,2,0:T(8,128)(2,1)S(1)}, bf16[1,32,1,512]{3,1,2,0:T(8,128)(2,1)}, u32[]{:S(2)}) copy-start(bf16[1,32,1,512]{3,1,2,0:T(8,128)(2,1)} %param.18) | copy-start | bytes 98308
  9.5 53.2 %copy-start.10 = (f32[1,128]{1,0:T(1,128)S(1)}, f32[1,128]{1,0:T(1,128)}, u32[]{:S(2)}) copy-start(f32[1,128]{1,0:T(1,128)} %param.23) | copy-start | bytes 1540
  9.5 53.5 %copy-start.11 = (f32[1,128]{1,0:T(1,128)S(1)}, f32[1,128]{1,0:T(1,128)}, u32[]{:S(2)}) copy-start(f32[1,128]{1,0:T(1,128)} %param.22) | copy-start | bytes 1540
  9.5 53.8 %copy-start.13 = (bf16[1,2,1024,1,128]{4,2,3,1,0:T(8,128)(2,1)S(1)}, bf16[1,2,1024,1,128]{4,2,3,1,0:T(8,128)(2,1)}, u32[]{:S(2)}) copy-start(bf16[1,2,1024,1,128]{4,2,3,1,0:T(8,128)(2,1)} %param.17) | copy-start | bytes 1572868
  9.5 29.6 %all-to-all-start = ((bf16[16,72,128]{2,1,0:T(8,128)(2,1)}), bf16[16,72,128]{2,1,0:T(8,128)(2,1)S(1)}, u32[]{:S(2)}, u32[]{:S(2)}) async-start(bf16[16,72,128]{2,1,0:T(8,128)(2,1)} %pad_maximum_fusion), calls=%async_computation | async-start | bytes 589824 | tf_op jit(solution)/shard_map/all_to_all | solution.py:27
  25.4 68.1 %all-gather.5.cloned.1.call-start = ((), (), s32[]{:S(2)}) async-start(), calls=%async_computation.8 | async-start | bytes 2506752 | tf_op jit(solution)/shard_map/all_gather | solution.py:60
  37.4 55.4 %copy-start.7 = (f32[1,2048]{1,0:T(1,128)S(1)}, f32[1,2048]{1,0:T(1,128)}, u32[]{:S(2)}) copy-start(f32[1,2048]{1,0:T(1,128)} %param.24) | copy-start | bytes 24580
  88.8 15.0 %all-to-all-start.4 = ((bf16[16,8,128]{2,1,0:T(8,128)(2,1)}), bf16[16,8,128]{2,1,0:T(8,128)(2,1)S(1)}, u32[]{:S(2)}, u32[]{:S(2)}) async-start(bf16[16,8,128]{2,1,0:T(8,128)(2,1)} %broadcast_in_dim.43), calls=%async_computation.4 | async-start | bytes 65536 | tf_op jit(solution)/shard_map/all_to_all | solution.py:27
  108.4 42.9 %copy-start.8 = (f32[2048]{0:T(1024)S(1)}, f32[2048]{0:T(1024)}, u32[]{:S(2)}) copy-start(f32[2048]{0:T(1024)} %param.28) | copy-start | bytes 24580
  108.5 42.9 %copy-start.1 = (bf16[2048,256]{1,0:T(8,128)(2,1)S(1)}, bf16[2048,256]{1,0:T(8,128)(2,1)}, u32[]{:S(2)}) copy-start(bf16[2048,256]{1,0:T(8,128)(2,1)} %param.29) | copy-start | bytes 3145732
  143.5 9.4 %collective-permute-start = (bf16[256,1024]{1,0:T(8,128)(2,1)S(1)}, bf16[256,1024]{1,0:T(8,128)(2,1)S(1)}, u32[]{:S(2)}, u32[]{:S(2)}) collective-permute-start(bf16[256,1024]{1,0:T(8,128)(2,1)S(1)} %bitcast.122), channel_id=1, source_target_pairs={{0,1},{1,0},{2,3},{3,2},{4,5},{5,4},{6,7},{7,6},{8,9},{9,8},{10,11... | collective-permute-start | bytes 1572872 | tf_op jit(solution)/shard_map/ppermute | solution.py:152
Sparse Core Ops, SparseCore 0:
  29.2 61.6 all-gather.4
where the time goes:
time: 162 us
  blocking collectives  95.2 us (59%)
  starting transfers between devices  27.3 us (17%)
  between operations  13.9 us (9%)
  waiting for transfers between devices  10.4 us (6%)
  local copies, waits for them, and re-layouts  6.97 us (4%)
  other arithmetic  5.44 us (3%)
  matrix products  2.44 us (2%)
    all_to_all x6, blocking collectives, swap(): return lax.all_to_all(values, axes, split_axis=0, concat_axis=0, tiled=True)  82 us
    all_to_all x2, starting transfers between devices, swap(): return lax.all_to_all(values, axes, split_axis=0, concat_axis=0, tiled=True)  19.4 us
    all_gather x1, blocking collectives, local(): qkv_block = lax.all_gather(w_qkv[0, :, 0], 'y', axis=0, tiled=True)  10.4 us
    all_to_all x2, waiting for transfers between devices, swap(): return lax.all_to_all(values, axes, split_axis=0, concat_axis=0, tiled=True)  9.26 us
    ppermute x1, starting transfers between devices, local(): far = lax.ppermute(near, 'c', [(0, 1), (1, 0)])  7.85 us
  transfers between devices with their start and end apart: 4, of which 3 were waited for; matrix products, arithmetic and copies ran while one was open for 5% of the time, Pallas kernels for 0%

commit v1 on v0

--- a/solution.py
+++ b/solution.py
@@ -58,7 +58,9 @@
     ix, ic = (lax.axis_index("x"), lax.axis_index("c"))
     ffn = jnp.concatenate([w_gate[0].T, w_up[0].T, w_down[0]], axis=0)
     ffn = lax.all_gather(ffn, ("y", "x"), axis=0).reshape(Y, X, -1, seg)
-    qkv_block = lax.all_gather(w_qkv[0, :, 0], "y", axis=0, tiled=True)
+    block_2 = w_qkv[0, :, 0]
+    repeated = jnp.stack([block_2] * lax.axis_size("y"))
+    qkv_block = jnp.concatenate(lax.all_to_all(repeated, "y", 0, 0), axis=0)
     positions = lax.dynamic_slice_in_dim(lengths, req * rows, rows)
     starts = jnp.cumsum(positions) - positions
     limits = starts + positions

time: 162 us -> 170 us (1.049)
  waiting for transfers between devices: 10.4 us -> 21.2 us
  blocking collectives: 95.2 us -> 85.3 us
  starting transfers between devices: 27.3 us -> 31.3 us
  local copies, waits for them, and re-layouts: 6.97 us -> 9.04 us
    all_to_all x2, waiting for transfers between devices: 9.26 us -> 20.1 us  [swap(): return lax.all_to_all(values, axes, split_axis=0, concat_axis=0, tiled=True)]
    all_gather x1 -> x0, blocking collectives: 10.4 us -> none  [local(): qkv_block = lax.all_gather(w_qkv[0, :, 0], 'y', axis=0, tiled=True)]
    all_to_all x0 -> x1, starting transfers between devices: none -> 5.01 us  [local(): qkv_block = jnp.concatenate(lax.all_to_all(repeated, 'y', 0, 0), axis=0)]
    another operation x1 -> x2, local copies, waits for them, and re-layouts: 0.08 us -> 2.22 us  [the longest x1 1.46 us: local(): repeated = jnp.stack([block_2] * lax.axis_size('y'))]
  transfers between devices with their start and end apart: 4 -> 5, of which waited for: 3 -> 3; matrix products, arithmetic and copies ran while one was open for 5% -> 7% of each run, Pallas kernels for 0% -> 0%
where the time goes in v1:
time: 170 us; the launch traced here: 169 us
  blocking collectives  85.3 us (50%)
  starting transfers between devices  31.3 us (18%)
  waiting for transfers between devices  21.2 us (12%)
  between operations  13.8 us (8%)
  local copies, waits for them, and re-layouts  9.04 us (5%)
  other arithmetic  6.29 us (4%)
  matrix products  2.45 us (1%)
    all_to_all x6, blocking collectives, swap(): return lax.all_to_all(values, axes, split_axis=0, concat_axis=0, tiled=True)  82.4 us
    all_to_all x2, waiting for transfers between devices, swap(): return lax.all_to_all(values, axes, split_axis=0, concat_axis=0, tiled=True)  20.1 us
    all_to_all x2, starting transfers between devices, swap(): return lax.all_to_all(values, axes, split_axis=0, concat_axis=0, tiled=True)  18.4 us
    ppermute x1, starting transfers between devices, local(): far = lax.ppermute(near, 'c', [(0, 1), (1, 0)])  7.88 us
    all_to_all x1, starting transfers between devices, local(): qkv_block = jnp.concatenate(lax.all_to_all(repeated, 'y', 0, 0), axis=0)  5.01 us
  transfers between devices with their start and end apart: 5, of which 3 were waited for; matrix products, arithmetic and copies ran while one was open for 7% of the time, Pallas kernels for 0%

profile of v1, /device:TPU:1, one launch (start us, length us, event | category | flops | bytes accessed | tf_op | source)
XLA Modules:
  0.0 169.4 jit_solution(398655541406828810)
XLA Ops:
  6.5 1.5 stack.3
  8.0 5.0 %all-to-all-start.1 = ((bf16[4,32,512]{2,1,0:T(8,128)(2,1)}), bf16[4,32,512]{2,1,0:T(8,128)(2,1)S(1)}, u32[]{:S(2)}, u32[]{:S(2)}) async-start(bf16[4,32,512]{2,1,0:T(8,128)(2,1)} %stack.3), calls=%async_computation.1 | async-start | bytes 262144 | tf_op jit(solution)/shard_map/all_to_all | solution.py:63
  13.0 1.5 pad_maximum_fusion.1
  14.6 0.7 fusion.47
  15.3 0.8 fusion.26
  16.1 0.1 reshape.226
  16.3 0.1 reshape.227
  16.4 0.8 dynamic-slice_bitcast_fusion
  17.2 0.2 reduce-window.8
  17.3 0.1 pad.10.clone
  17.5 0.8 pad_maximum_fusion
  18.4 14.9 %all-to-all-start = ((bf16[16,72,128]{2,1,0:T(8,128)(2,1)}), bf16[16,72,128]{2,1,0:T(8,128)(2,1)S(1)}, u32[]{:S(2)}, u32[]{:S(2)}) async-start(bf16[16,72,128]{2,1,0:T(8,128)(2,1)} %pad_maximum_fusion), calls=%async_computation | async-start | bytes 589824 | tf_op jit(solution)/shard_map/all_to_all | solution.py:27
  33.3 0.1 bitcast_subtract_fusion
  33.4 0.1 multiply_sine_fusion
  33.5 0.1 fusion.37
  33.7 0.2 fusion.10
  33.9 12.5 %all-to-all-done = bf16[16,72,128]{2,1,0:T(8,128)(2,1)S(1)} async-done(((bf16[16,72,128]{2,1,0:T(8,128)(2,1)}), bf16[16,72,128]{2,1,0:T(8,128)(2,1)S(1)}, u32[]{:S(2)}, u32[]{:S(2)}) %all-to-all-start) | async-done | bytes 294944 | tf_op jit(solution)/shard_map/all_to_all | solution.py:27
  46.5 0.1 convolution_convert_fusion
  46.7 23.3 %all_to_all.45 = bf16[16,4,512]{2,1,0:T(4,128)(2,1)S(1)} all-to-all(bf16[16,4,512]{2,1,0:T(4,128)(2,1)S(1)} %reshape.234), channel_id=1, replica_groups=mesh['y'=4,'zh'=4,'zl'=4,'x'=4,'c'=2] {'zh','zl'}, dimensions={0} | all-to-all | bytes 131072 | tf_op jit(solution)/shard_map/all_to_all | solution.py:27
  70.1 0.1 broadcast_multiply_fusion
  70.1 0.1 multiply_reduce_fusion.3
  70.3 0.1 multiply_multiply_fusion.1
  70.3 0.1 subtract_convert_fusion.1
  70.4 0.1 maximum_convert_fusion
  70.5 0.1 multiply_reduce_fusion.2
  70.6 0.1 multiply_multiply_fusion
  70.7 0.1 subtract_convert_fusion
  70.7 0.2 multiply_reduce_fusion.1
  70.9 0.3 fusion.48
  71.3 0.2 fusion.7
  71.4 8.7 %all_to_all.46 = bf16[4,8,128]{2,1,0:T(8,128)(2,1)S(1)} all-to-all(bf16[4,8,128]{2,1,0:T(8,128)(2,1)S(1)} %broadcast_in_dim.42), channel_id=1, replica_groups=mesh['y'=4,'zh'=4,'zl'=4,'x'=4,'c'=2] {'y'}, dimensions={0} | all-to-all | bytes 16384 | tf_op jit(solution)/shard_map/all_to_all | solution.py:27
  80.1 0.2 convolution_bitcast_fusion.2
  80.4 15.6 %all_to_all.47 = f32[32,2,128]{2,1,0:T(2,128)S(1)} all-to-all(f32[32,2,128]{2,1,0:T(2,128)S(1)} %reshape.239), channel_id=1, replica_groups=mesh['y'=4,'zh'=4,'zl'=4,'x'=4,'c'=2] {'y','x','c'}, dimensions={0} | all-to-all | bytes 65536 | tf_op jit(solution)/shard_map/all_to_all | solution.py:27
  96.0 0.6 broadcast_in_dim.43
  96.6 3.5 %all-to-all-start.5 = ((bf16[16,8,128]{2,1,0:T(8,128)(2,1)}), bf16[16,8,128]{2,1,0:T(8,128)(2,1)S(1)}, u32[]{:S(2)}, u32[]{:S(2)}) async-start(bf16[16,8,128]{2,1,0:T(8,128)(2,1)} %broadcast_in_dim.43), calls=%async_computation.5 | async-start | bytes 65536 | tf_op jit(solution)/shard_map/all_to_all | solution.py:27
  100.1 0.5 broadcast.165
  100.7 0.6 reduce.12
  101.3 1.5 slice_bitcast_fusion
  102.8 1.2 slice.85
  104.1 7.5 %all-to-all-done.5 = bf16[16,8,128]{2,1,0:T(8,128)(2,1)S(1)} async-done(((bf16[16,8,128]{2,1,0:T(8,128)(2,1)}), bf16[16,8,128]{2,1,0:T(8,128)(2,1)S(1)}, u32[]{:S(2)}, u32[]{:S(2)}) %all-to-all-start.5) | async-done | bytes 32800 | tf_op jit(solution)/shard_map/all_to_all | solution.py:27
  111.6 0.2 multiply_reduce_fusion
  111.8 0.1 copy.64
  112.0 0.5 convolution_bitcast_fusion.1
  112.6 2.9 %all-gather.1 = f32[32,896]{1,0:T(8,128)S(1)} all-gather(f32[16,896]{1,0:T(8,128)S(1)} %pad_maximum_fusion.2), channel_id=3, replica_groups=mesh['y'=4,'zh'=4,'zl'=4,'x'=4,'c'=2] {'c'}, dimensions={0}, use_global_device_ids=true | all-gather | bytes 172032 | tf_op jit(solution)/shard_map/all_gather | solution.py:145
  115.5 0.2 fusion.40
  115.7 0.1 slice_multiply_fusion
  115.8 0.1 reshape.245
  115.9 0.1 fusion.46
  116.0 0.3 fusion.1
  116.3 7.4 %all_to_all.48 = bf16[4,16,8,128]{3,2,1,0:T(8,128)(2,1)S(1)} all-to-all(bf16[4,16,8,128]{3,2,1,0:T(8,128)(2,1)S(1)} %broadcast_in_dim.46), channel_id=1, replica_groups=mesh['y'=4,'zh'=4,'zl'=4,'x'=4,'c'=2] {'zl'}, dimensions={0} | all-to-all | bytes 262144 | tf_op jit(solution)/shard_map/all_to_all | solution.py:27
  123.8 15.6 %all_to_all.49 = bf16[4,16,8,128]{3,2,1,0:T(8,128)(2,1)S(1)} all-to-all(bf16[4,16,8,128]{3,2,1,0:T(8,128)(2,1)S(1)} %broadcast_in_dim.47), channel_id=1, replica_groups=mesh['y'=4,'zh'=4,'zl'=4,'x'=4,'c'=2] {'zh'}, dimensions={0} | all-to-all | bytes 262144 | tf_op jit(solution)/shard_map/all_to_all | solution.py:27
  139.5 11.8 %all_to_all.50 = bf16[16,16,1024]{2,1,0:T(8,128)(2,1)S(1)} all-to-all(bf16[16,16,1024]{2,1,0:T(8,128)(2,1)S(1)} %broadcast_in_dim.49), channel_id=1, replica_groups=mesh['y'=4,'zh'=4,'zl'=4,'x'=4,'c'=2] {'y','x'}, dimensions={0} | all-to-all | bytes 1048576 | tf_op jit(solution)/shard_map/all_to_all | solution.py:27
  151.2 7.9 %collective-permute-start = (bf16[256,1024]{1,0:T(8,128)(2,1)S(1)}, bf16[256,1024]{1,0:T(8,128)(2,1)S(1)}, u32[]{:S(2)}, u32[]{:S(2)}) collective-permute-start(bf16[256,1024]{1,0:T(8,128)(2,1)S(1)} %bitcast.123), channel_id=1, source_target_pairs={{0,1},{1,0},{2,3},{3,2},{4,5},{5,4},{6,7},{7,6},{8,9},{9,8},{10,11... | collective-permute-start | bytes 1572872 | tf_op jit(solution)/shard_map/ppermute | solution.py:154
  159.2 0.1 constant_dynamic-slice_fusion
  159.3 0.2 fusion.11
  159.4 0.1 reduce_sum.138
  159.5 1.1 collective-permute-done
  160.6 0.2 fusion.14
  160.8 0.1 reduce_sum.137
  160.9 0.2 fusion.13
  161.1 0.3 fusion.49
  161.4 0.4 fusion
  161.8 0.1 copy.69
  161.9 0.7 reshape.252
  (70 shorter events, 0.9 us)
Async XLA Ops:
  6.5 27.2 %copy-start = (bf16[1,2048,2]{1,2,0:T(2,128)(2,1)S(1)}, bf16[1,2048,2]{1,2,0:T(2,128)(2,1)}, u32[]{:S(2)}) copy-start(bf16[1,2048,2]{1,2,0:T(2,128)(2,1)} %param.19) | copy-start | bytes 24580
  6.5 27.1 %copy-start.2 = (bf16[4,2048]{1,0:T(4,128)(2,1)S(1)}, bf16[4,2048]{1,0:T(4,128)(2,1)}, u32[]{:S(2)}) copy-start(bf16[4,2048]{1,0:T(4,128)(2,1)} %param.15) | copy-start | bytes 49156
  6.5 27.2 %copy-start.5 = (f32[1,2048]{1,0:T(1,128)S(1)}, f32[1,2048]{1,0:T(1,128)}, u32[]{:S(2)}) copy-start(f32[1,2048]{1,0:T(1,128)} %param.21) | copy-start | bytes 24580
  6.5 26.8 %copy-start.8 = (s32[256]{0:T(256)S(1)}, s32[256]{0:T(256)}, u32[]{:S(2)}) copy-start(s32[256]{0:T(256)} %param.16) | copy-start | bytes 3076
  8.0 10.4 %all-to-all-start.1 = ((bf16[4,32,512]{2,1,0:T(8,128)(2,1)}), bf16[4,32,512]{2,1,0:T(8,128)(2,1)S(1)}, u32[]{:S(2)}, u32[]{:S(2)}) async-start(bf16[4,32,512]{2,1,0:T(8,128)(2,1)} %stack.3), calls=%async_computation.1 | async-start | bytes 262144 | tf_op jit(solution)/shard_map/all_to_all | solution.py:63
  13.0 88.3 %all-gather.4.cloned.1.call-start = ((), (), s32[]{:S(2)}) async-start(), calls=%async_computation.9 | async-start | bytes 2506752 | tf_op jit(solution)/shard_map/all_gather | solution.py:60
  17.4 52.8 %copy-start.6 = (f32[1,128]{1,0:T(1,128)S(1)}, f32[1,128]{1,0:T(1,128)}, u32[]{:S(2)}) copy-start(f32[1,128]{1,0:T(1,128)} %param.23) | copy-start | bytes 1540
  17.5 53.1 %copy-start.7 = (f32[1,128]{1,0:T(1,128)S(1)}, f32[1,128]{1,0:T(1,128)}, u32[]{:S(2)}) copy-start(f32[1,128]{1,0:T(1,128)} %param.22) | copy-start | bytes 1540
  17.5 53.4 %copy-start.9 = (bf16[1,2,1024,1,128]{4,2,3,1,0:T(8,128)(2,1)S(1)}, bf16[1,2,1024,1,128]{4,2,3,1,0:T(8,128)(2,1)}, u32[]{:S(2)}) copy-start(bf16[1,2,1024,1,128]{4,2,3,1,0:T(8,128)(2,1)} %param.17) | copy-start | bytes 1572868
  18.4 28.1 %all-to-all-start = ((bf16[16,72,128]{2,1,0:T(8,128)(2,1)}), bf16[16,72,128]{2,1,0:T(8,128)(2,1)S(1)}, u32[]{:S(2)}, u32[]{:S(2)}) async-start(bf16[16,72,128]{2,1,0:T(8,128)(2,1)} %pad_maximum_fusion), calls=%async_computation | async-start | bytes 589824 | tf_op jit(solution)/shard_map/all_to_all | solution.py:27
  33.9 66.7 %copy-start.3 = (f32[1,2048]{1,0:T(1,128)S(1)}, f32[1,2048]{1,0:T(1,128)}, u32[]{:S(2)}) copy-start(f32[1,2048]{1,0:T(1,128)} %param.24) | copy-start | bytes 24580
  96.6 15.0 %all-to-all-start.5 = ((bf16[16,8,128]{2,1,0:T(8,128)(2,1)}), bf16[16,8,128]{2,1,0:T(8,128)(2,1)S(1)}, u32[]{:S(2)}, u32[]{:S(2)}) async-start(bf16[16,8,128]{2,1,0:T(8,128)(2,1)} %broadcast_in_dim.43), calls=%async_computation.5 | async-start | bytes 65536 | tf_op jit(solution)/shard_map/all_to_all | solution.py:27
  116.2 42.9 %copy-start.4 = (f32[2048]{0:T(1024)S(1)}, f32[2048]{0:T(1024)}, u32[]{:S(2)}) copy-start(f32[2048]{0:T(1024)} %param.28) | copy-start | bytes 24580
  116.3 42.9 %copy-start.1 = (bf16[2048,256]{1,0:T(8,128)(2,1)S(1)}, bf16[2048,256]{1,0:T(8,128)(2,1)}, u32[]{:S(2)}) copy-start(bf16[2048,256]{1,0:T(8,128)(2,1)} %param.29) | copy-start | bytes 3145732
  151.2 9.4 %collective-permute-start = (bf16[256,1024]{1,0:T(8,128)(2,1)S(1)}, bf16[256,1024]{1,0:T(8,128)(2,1)S(1)}, u32[]{:S(2)}, u32[]{:S(2)}) collective-permute-start(bf16[256,1024]{1,0:T(8,128)(2,1)S(1)} %bitcast.123), channel_id=1, source_target_pairs={{0,1},{1,0},{2,3},{3,2},{4,5},{5,4},{6,7},{7,6},{8,9},{9,8},{10,11... | collective-permute-start | bytes 1572872 | tf_op jit(solution)/shard_map/ppermute | solution.py:154
Sparse Core Ops, SparseCore 0:
  16.8 65.0 all-gather.3
